TPU v7x, 32 devices: a whole 2x2x4 slice. The times are simulated.
32 devices in a mesh: grp: 4 (over z), pen: 8 (over y, x, core).
Axes of the slice: x: 2, y: 2, z: 4, core: 2. Of those that a mesh axis runs over, the one named last changes fastest.
Arguments:
- cell_offsets: int32 [2, 1048576], P(None, ('grp', 'pen')), may hold values from 0 to 1
- cell_z: int32 [1048576], P(('grp', 'pen')), may hold values from 0 to 255
- frac: float32 [3, 1048576], P(None, ('grp', 'pen')), may hold values from 0 to 1
- charges: float32 [1048576], P(('grp', 'pen')), may hold values from -4 to 4
- tile_counts: int32 [16384], P(('grp', 'pen')), may hold values from 16 to 64, as said below
Outputs:
- forces: float32 [3, 1048576], P(None, ('grp', 'pen'))
- energy: float32 [], replicated
Inputs may be any that keep to these rules, and one draw needn't show every extreme that they name: `tile_counts`: live slots of each tile; some tile holds 64.
All inputs are finite; a program needn't handle non-finite values.
Results may differ from a plain program's by a relative error of at most 0.0003.
Values sent between devices are 32-bit elements; how exact they have to be, the bound alone decides.
A program may use at most 256 MiB of HBM per device.

v0:
```python
import math
import jax
import jax.numpy as jnp
from jax import lax
from jax.sharding import PartitionSpec as P

KX = 256
KY = 256
KZ = 256
ATOMS = 1048576
ewald_split = 0.6
highest = lax.Precision.HIGHEST


def shifted(block, axis, distance):
    devices = range(lax.axis_size(axis))
    route = [((i - distance) % len(devices), i) for i in devices]
    return lax.ppermute(block, axis, route)


def spline_rows(fracs):
    values = [jnp.ones_like(fracs)]
    fifth = values
    for order in range(2, 7):
        nxt = []
        for j in range(order):
            term = jnp.zeros_like(fracs)
            if j >= 1:
                term = values[j - 1] * (fracs + order - 1 - j)
            if j <= order - 2:
                term = term + values[j] * (1.0 - fracs + j)
            nxt.append(term / (order - 1))
        if order == 5:
            fifth = nxt
        values = nxt
    slopes = []
    for j in range(6):
        term = jnp.zeros_like(fracs)
        if j >= 1:
            term = fifth[j - 1]
        if j <= 4:
            term = term - fifth[j]
        slopes.append(term)
    return (values, slopes)


def tile_weights(offsets, zcell, fracs, charge, counts, size_z):
    slots = charge.shape[-1]
    live = (jnp.arange(slots, dtype=jnp.int32) < counts[..., None]).astype(jnp.float32)
    live_q = charge * live
    theta_x, slope_x = spline_rows(fracs[0])
    theta_y, slope_y = spline_rows(fracs[1])
    theta_z, slope_z = spline_rows(fracs[2])
    footing = jnp.arange(8, dtype=jnp.int32)[:, None]
    cells = jnp.arange(size_z, dtype=jnp.int32)
    weight_x = 0.0
    grade_x = 0.0
    weight_y = 0.0
    grade_y = 0.0
    weight_z = 0.0
    grade_z = 0.0
    for j in range(6):
        hit_x = (footing == offsets[0][..., None, :] + j).astype(jnp.float32)
        hit_y = (footing == offsets[1][..., None, :] + j).astype(jnp.float32)
        hit_z = (cells == (zcell[..., :, None] + j) % size_z).astype(jnp.float32)
        weight_x = weight_x + theta_x[j][..., None, :] * hit_x
        grade_x = grade_x + slope_x[j][..., None, :] * hit_x
        weight_y = weight_y + theta_y[j][..., None, :] * hit_y
        grade_y = grade_y + slope_y[j][..., None, :] * hit_y
        weight_z = weight_z + theta_z[j][..., :, None] * hit_z
        grade_z = grade_z + slope_z[j][..., :, None] * hit_z
    return (weight_x, grade_x, weight_y, grade_y, weight_z, grade_z, live_q)


def modulus(index, length):
    coeffs = (1.0 / 120.0, 26.0 / 120.0, 66.0 / 120.0, 26.0 / 120.0, 1.0 / 120.0)
    real_part = 0.0
    imag_part = 0.0
    for j in range(5):
        angle = (index * j % length).astype(jnp.float32) * (2.0 * math.pi / length)
        real_part = real_part + coeffs[j] * jnp.cos(angle)
        imag_part = imag_part + coeffs[j] * jnp.sin(angle)
    return real_part * real_part + imag_part * imag_part


def influence(index_x, index_y, index_z):
    freq_x = jnp.where(2 * index_x < KX, index_x, index_x - KX).astype(jnp.float32) / KX
    freq_y = jnp.where(2 * index_y < KY, index_y, index_y - KY).astype(jnp.float32) / KY
    freq_z = jnp.where(2 * index_z < KZ, index_z, index_z - KZ).astype(jnp.float32) / KZ
    square = freq_x * freq_x + freq_y * freq_y + freq_z * freq_z
    safe = jnp.where(square > 0, square, 1.0)
    volume = float(KX * KY * KZ)
    value = jnp.exp(-math.pi**2 * safe / ewald_split**2) / (math.pi * volume * safe)
    value = value / (modulus(index_x, KX) * modulus(index_y, KY) * modulus(index_z, KZ))
    return jnp.where(square > 0, value, 0.0)


def dft_tables(length):
    index = jnp.arange(length, dtype=jnp.int32)
    angle = (index[:, None] * index[None, :] % length).astype(jnp.float32) * (
        2.0 * math.pi / length
    )
    return (jnp.cos(angle), jnp.sin(angle))


def z_slots(groups):
    planes = KZ // (2 * groups) + 1
    owner = jnp.arange(groups, dtype=jnp.int32)[:, None]
    within = jnp.arange(planes, dtype=jnp.int32)[None, :]
    ordinary = owner * (planes - 1) + within
    frequency = jnp.where(within < planes - 1, ordinary, jnp.where(owner == 0, KZ // 2, 0))
    plane_weight = jnp.where(
        within < planes - 1, jnp.where(frequency == 0, 1.0, 2.0), jnp.where(owner == 0, 1.0, 0.0)
    )
    frequency = frequency.reshape(-1)
    plane_weight = plane_weight.reshape(-1).astype(jnp.float32)
    position = jnp.arange(KZ, dtype=jnp.int32)
    angle = (frequency[:, None] * position[None, :] % KZ).astype(jnp.float32) * (2.0 * math.pi / KZ)
    usable = (plane_weight > 0).astype(jnp.float32)[:, None]
    return (planes, frequency, plane_weight, jnp.cos(angle) * usable, jnp.sin(angle) * usable)


def forward_complex(data, cos_table, sin_table, shape, axis):
    direct = jnp.dot(cos_table, data, precision=highest).reshape(shape)
    other = jnp.dot(sin_table, data, precision=highest).reshape(shape)
    real_part = jnp.take(direct, 0, axis=axis) + jnp.take(other, 1, axis=axis)
    imag_part = jnp.take(direct, 1, axis=axis) - jnp.take(other, 0, axis=axis)
    return (real_part, imag_part)


def inverse_complex(data, cos_table, sin_table, shape, axis):
    direct = jnp.dot(cos_table, data, precision=highest).reshape(shape)
    other = jnp.dot(sin_table, data, precision=highest).reshape(shape)
    real_part = jnp.take(direct, 0, axis=axis) - jnp.take(other, 1, axis=axis)
    imag_part = jnp.take(other, 0, axis=axis) + jnp.take(direct, 1, axis=axis)
    return (real_part, imag_part)


def spectrum_pen_first(grid, block_x, block_y):
    cos_x, sin_x = dft_tables(KX)
    cos_y, sin_y = dft_tables(KY)
    planes, frequency, plane_weight, cos_z, sin_z = z_slots(lax.axis_size("pen"))
    slot_total = cos_z.shape[0]
    lines = KY // lax.axis_size("grp")
    real_z = jnp.einsum("xyz,kz->ykx", grid, cos_z, precision=highest)
    imag_z = -jnp.einsum("xyz,kz->ykx", grid, sin_z, precision=highest)
    outgoing = jnp.stack([real_z, imag_z], axis=2).reshape(block_y, slot_total * 2 * block_x)
    columns = lax.all_to_all(outgoing, "pen", split_axis=1, concat_axis=0, tiled=True)
    real_y, imag_y = forward_complex(columns, cos_y, sin_y, (KY, planes, 2, block_x), 2)
    sectioned = jnp.transpose(jnp.stack([real_y, imag_y], axis=-1), (2, 0, 1, 3)).reshape(
        block_x, KY * planes * 2
    )
    rows = lax.all_to_all(sectioned, "grp", split_axis=1, concat_axis=0, tiled=True)
    real_x, imag_x = forward_complex(rows, cos_x, sin_x, (KX, lines, planes, 2), 3)
    first = lax.axis_index("pen") * planes
    index_x = jnp.arange(KX, dtype=jnp.int32)[:, None, None]
    index_y = lax.axis_index("grp") * lines + jnp.arange(lines, dtype=jnp.int32)[None, :, None]
    index_z = lax.dynamic_slice_in_dim(frequency, first, planes)[None, None, :]
    local_weight = lax.dynamic_slice_in_dim(plane_weight, first, planes)[None, None, :]
    kernel = influence(index_x, index_y, index_z)
    spectral = 0.5 * jnp.sum(local_weight * kernel * (real_x * real_x + imag_x * imag_x))
    scaled = jnp.stack([kernel * real_x, kernel * imag_x], axis=-1).reshape(KX, lines * planes * 2)
    real_b, imag_b = inverse_complex(scaled, cos_x, sin_x, (KX, lines, planes, 2), 3)
    returning = jnp.stack([real_b, imag_b], axis=-1).reshape(KX, lines * planes * 2)
    rows_home = lax.all_to_all(returning, "grp", split_axis=0, concat_axis=1, tiled=True)
    rows_home = jnp.transpose(rows_home.reshape(block_x, KY, planes, 2), (1, 2, 3, 0)).reshape(
        KY, planes * 2 * block_x
    )
    real_c, imag_c = inverse_complex(rows_home, cos_y, sin_y, (KY, planes, 2, block_x), 2)
    leaving = jnp.stack([real_c, imag_c], axis=2).reshape(KY, planes * 2 * block_x)
    home = lax.all_to_all(leaving, "pen", split_axis=0, concat_axis=1, tiled=True).reshape(
        block_y, slot_total, 2, block_x
    )
    potential = jnp.einsum(
        "ykx,kz->xyz", home[:, :, 0], plane_weight[:, None] * cos_z, precision=highest
    )
    potential = potential - jnp.einsum(
        "ykx,kz->xyz", home[:, :, 1], plane_weight[:, None] * sin_z, precision=highest
    )
    return (potential, spectral)


def place_tiles(spread, tiles_x, tiles_y):
    shaped = spread.reshape(tiles_x, tiles_y, 4, 2, 4, 2, KZ)
    total = 0.0
    for i in range(4):
        for j in range(4):
            part = jnp.transpose(shaped[:, :, i, :, j], (0, 2, 1, 3, 4)).reshape(
                2 * tiles_x, 2 * tiles_y, KZ
            )
            total = total + jnp.pad(part, ((2 * i, 6 - 2 * i), (2 * j, 6 - 2 * j), (0, 0)))
    return total


def gather_tiles(extended, tiles_x, tiles_y):
    blocks = []
    for i in range(4):
        members = []
        for j in range(4):
            part = extended[2 * i : 2 * i + 2 * tiles_x, 2 * j : 2 * j + 2 * tiles_y]
            part = part.reshape(tiles_x, 2, tiles_y, 2, KZ)
            members.append(jnp.transpose(part, (0, 2, 1, 3, 4)))
        blocks.append(jnp.stack(members, axis=3))
    return jnp.stack(blocks, axis=2).reshape(tiles_x, tiles_y, 64, KZ)


def local(cell_offsets, cell_z, frac, charges, tile_counts):
    block_x = KX // lax.axis_size("grp")
    block_y = KY // lax.axis_size("pen")
    tiles_x = block_x // 2
    tiles_y = block_y // 2
    slots = charges.shape[0] // (tiles_x * tiles_y)
    offsets = cell_offsets.reshape(2, tiles_x, tiles_y, slots)
    zcell = cell_z.reshape(tiles_x, tiles_y, slots)
    fracs = frac.reshape(3, tiles_x, tiles_y, slots)
    charge = charges.reshape(tiles_x, tiles_y, slots)
    counts = tile_counts.reshape(tiles_x, tiles_y)
    weight_x, grade_x, weight_y, grade_y, weight_z, grade_z, live_q = tile_weights(
        offsets, zcell, fracs, charge, counts, KZ
    )
    pair = weight_x[..., :, None, :] * weight_y[..., None, :, :] * live_q[..., None, None, :]
    pair = pair.reshape(tiles_x, tiles_y, 64, slots)
    spread = jnp.einsum("abfs,absz->abfz", pair, weight_z, precision=highest)
    padded = place_tiles(spread, tiles_x, tiles_y)
    rim_y = shifted(padded[: block_x + 5, block_y : block_y + 5], "pen", 1)
    merged = padded[: block_x + 5, :block_y].at[:, :5].add(rim_y)
    rim_x = shifted(merged[block_x : block_x + 5], "grp", 1)
    grid = merged[:block_x].at[:5].add(rim_x)
    potential, spectral = spectrum_pen_first(grid, block_x, block_y)
    upper = shifted(potential[:5], "grp", -1)
    ext_x = jnp.concatenate([potential, upper, jnp.zeros((1, block_y, KZ), jnp.float32)], axis=0)
    beside = shifted(ext_x[:, :5], "pen", -1)
    extended = jnp.concatenate(
        [ext_x, beside, jnp.zeros((block_x + 6, 1, KZ), jnp.float32)], axis=1
    )
    footing = gather_tiles(extended, tiles_x, tiles_y)
    main = jnp.einsum("abfz,absz->abfs", footing, weight_z, precision=highest).reshape(
        tiles_x, tiles_y, 8, 8, slots
    )
    tilt = jnp.einsum("abfz,absz->abfs", footing, grade_z, precision=highest).reshape(
        tiles_x, tiles_y, 8, 8, slots
    )
    force_x = -live_q * jnp.einsum(
        "abxs,abys,abxys->abs", grade_x, weight_y, main, precision=highest
    )
    force_y = -live_q * jnp.einsum(
        "abxs,abys,abxys->abs", weight_x, grade_y, main, precision=highest
    )
    force_z = -live_q * jnp.einsum(
        "abxs,abys,abxys->abs", weight_x, weight_y, tilt, precision=highest
    )
    total = lax.psum(spectral, ("grp", "pen"))
    forces = jnp.stack([force_x, force_y, force_z], axis=0).reshape(3, tiles_x * tiles_y * slots)
    return (forces, total / ATOMS)


def solution(mesh):
    in_specs = (
        P(None, ("grp", "pen")),
        P(("grp", "pen")),
        P(None, ("grp", "pen")),
        P(("grp", "pen")),
        P(("grp", "pen")),
    )
    out_specs = (P(None, ("grp", "pen")), P())
    return jax.shard_map(local, mesh=mesh, in_specs=in_specs, out_specs=out_specs, check_vma=False)
```

profile of v0, /device:TPU:0, one launch (start us, length us, event | category | flops | bytes accessed | tf_op | source)
XLA Modules:
  0.0 1138.8 jit_solution(11327651914012425456)
XLA Ops:
  22.6 140.7 %fusion.15 = f32[32,16,64,256]{3,2,1,0:T(8,128)} fusion(f32[32,16,64]{2,1,0:T(8,128)S(1)} %copy-done.60, s32[32,16,64]{2,1,0:T(8,128)S(1)} %get-tuple-element.184, f32[32,16,64]{2,1,0:T(8,128)S(1)} %copy-done.58, s32[32,16,64]{2,1,0:T(8,128)S(1)} %get-tuple-element.183, f32[32,16,64]{2,1,0:T(8,128)S(1)} %copy-done.54, ...), kind=kOutput, calls=%fused_computation.27 | convolution fusion | flops 6589251584 | bytes 37355520 | tf_op jit(solution)/shard_map/abfs,absz->abfz/dot_general | solution.py:223
  163.2 39.0 %reshape.1907 = f32[32,16,4,2,4,2,256]{6,5,4,3,2,1,0:T(2,128)} reshape(f32[32,16,64,256]{3,2,1,0:T(8,128)} %fusion.15) | data formatting | bytes 67108864 | tf_op jit(solution)/shard_map/reshape | solution.py:184
  202.2 25.3 %slice_bitcast_fusion.15 = (f32[32,2,16,2,256]{4,3,1,2,0:T(2,128)S(1)}, f32[32,2,16,2,256]{4,3,1,2,0:T(2,128)S(1)}, f32[32,2,16,2,256]{4,3,1,2,0:T(2,128)}, f32[...) fusion(f32[32,16,4,2,4,2,256]{6,5,4,3,2,1,0:T(2,128)} %reshape.1907), kind=kLoop, calls=%fused_computation.93 | loop fusion | bytes 67108864 | tf_op jit(solution)/shard_map/transpose | solution.py:188
  241.3 4.1 copy.276
  256.9 4.1 copy.278
  287.6 4.0 copy.282
  291.7 4.0 reshape.1916
  303.4 4.1 copy.284
  318.8 4.1 copy.286
  348.2 12.9 %pad_add_fusion = f32[70,38,256]{2,0,1:T(8,128)S(1)} fusion(f32[64,32,256]{2,0,1:T(8,128)} %reshape.1923, f32[64,32,256]{2,0,1:T(8,128)} %reshape.1922, f32[64,32,256]{2,0,1:T(8,128)} %reshape.1921, f32[64,32,256]{2,0,1:T(8,128)} %reshape.1920, f32[64,32,256]{2,0,1:T(8,128)} %reshape.1919, f32[64,32,256]{2,0,1:T(8,128)} %reshape.1918, ...), kind=kLoop, calls=%fused_computation.52 | loop fusion | flops 10214400 | bytes 36278272 | tf_op jit(solution)/shard_map/add | solution.py:191
  365.0 4.7 collective-permute-done
  375.6 5.0 collective-permute-done.1
  389.0 7.5 copy.290
  396.5 4.6 all_to_all.52
  401.6 31.4 %all_to_all.70 = f32[32,8,2176]{2,0,1:T(8,128)} all-to-all(f32[32,8,2176]{2,0,1:T(8,128)S(1)} %copy.291), channel_id=1, replica_groups=mesh['grp'=4,'pen'=8] {'pen'}, dimensions={1} | all-to-all | bytes 4456448 | tf_op jit(solution)/shard_map/all_to_all | solution.py:148
  441.5 5.1 copy.296
  446.6 5.1 copy.297
  456.4 50.4 %all-to-all-done.1 = f32[64,4,2176]{2,0,1:T(8,128)S(1)} async-done(((f32[64,4,2176]{2,0,1:T(8,128)}), f32[64,4,2176]{2,0,1:T(8,128)S(1)}, u32[]{:S(2)}, u32[]{:S(2)}) %all-to-all-start.1) | async-done | bytes 2228256 | tf_op jit(solution)/shard_map/all_to_all | solution.py:153
  535.2 4.9 all_to_all.60
  540.0 4.5 copy.311
  544.6 54.0 %all_to_all.71 = f32[4,64,2176]{2,1,0:T(8,128)} all-to-all(f32[4,64,2176]{2,1,0:T(8,128)S(1)} %copy.311), channel_id=1, replica_groups=mesh['grp'=4,'pen'=8] {'grp'}, dimensions={0} | all-to-all | bytes 4456448 | tf_op jit(solution)/shard_map/all_to_all | solution.py:165
  598.6 4.7 copy.312
  603.4 7.0 copy.372
  610.4 6.1 copy.313
  616.5 4.6 fusion.36
  624.8 5.1 copy.317
  629.9 4.6 all_to_all.63
  634.5 30.8 %all_to_all.72 = f32[8,32,2176]{2,1,0:T(8,128)S(1)} all-to-all(f32[8,32,2176]{2,1,0:T(8,128)S(1)} %all_to_all.63), channel_id=1, replica_groups=mesh['grp'=4,'pen'=8] {'pen'}, dimensions={0} | all-to-all | bytes 4456448 | tf_op jit(solution)/shard_map/all_to_all | solution.py:171
  666.6 4.1 reshape.1927
  670.7 8.8 fusion.280
  679.5 5.8 copy.378
  685.4 5.3 fusion.141
  690.6 4.5 copy.377
  695.1 4.2 fusion.143
  701.5 55.4 %select_add_fusion.1.clone.4 = f32[32,16,64,256]{3,2,1,0:T(8,128)} fusion(f32[32,16,64]{2,1,0:T(8,128)S(1)} %copy-done.61, s32[32,16,64]{2,1,0:T(8,128)S(1)} %copy-done.43, f32[32,16,64]{2,1,0:T(8,128)S(1)} %copy-done.59, s32[32,16,64]{2,1,0:T(8,128)S(1)} %copy-done.41, f32[32,16,64]{2,1,0:T(8,128)S(1)} %copy-done.55, ...), kind=kLoop, calls=%fused_computation.13.clone.clone.clone.clone.1 | loop fusion | flops 142606336 | bytes 35127296 | tf_op jit(solution)/shard_map/abxs,abys,abxys->abs/dot_general | solution.py:243
  758.3 55.3 %fusion.294 = f32[32,16,64,256]{3,2,1,0:T(8,128)} fusion(f32[32,16,64]{2,1,0:T(8,128)S(1)} %copy-done.53, f32[32,16,64]{2,1,0:T(8,128)S(1)} %copy-done.51, f32[32,16,64]{2,1,0:T(8,128)S(1)} %copy-done.50, f32[32,16,64]{2,1,0:T(8,128)S(1)} %copy-done.52, f32[32,16,64]{2,1,0:T(8,128)S(1)} %copy-done.49, f32[32,16,64]{2,1,0:T(8,128)S(1)} %copy-done.48, ...), kind=kLoop, calls=%fused_computation.2.clone.clone.clone.1 | loop fusion | flops 142606336 | bytes 35127296 | tf_op jit(solution)/shard_map/abfz,absz->abfs/dot_general | solution.py:240
  814.3 38.4 %psum.7 = f32[]{:T(128)} all-reduce(f32[]{:T(128)S(6)} %mul_shard_map.3), channel_id=1, replica_groups=mesh['grp'=4,'pen'=8] {'grp','pen'}, use_global_device_ids=true, to_apply=%region_1.6 | all-reduce | flops 1 | bytes 8 | tf_op jit(solution)/shard_map/psum | solution.py:252
  869.1 6.2 fusion.282
  916.1 6.8 maximum_bitcast_fusion
  922.9 4.5 maximum_bitcast_fusion.1
  927.5 5.3 maximum_bitcast_fusion.2
  933.8 5.2 maximum_bitcast_fusion.3
  939.1 18.5 %pad_maximum_fusion = f32[32,16,4,2,4,2,256]{6,3,0,5,1,4,2:T(2,128)} fusion(f32[32,16,1,2,4,2,256]{6,3,0,5,1,4,2:T(2,128)} %maximum_bitcast_fusion.3, f32[32,16,1,2,4,2,256]{6,3,0,5,1,4,2:T(2,128)} %maximum_bitcast_fusion.2, f32[32,16,1,2,4,2,256]{6,3,0,5,1,4,2:T(2,128)S(1)} %maximum_bitcast_fusion.1, f32[32,16,1,2,4,2,256]{6,3,0,5,1,4,2:T(2,128)S(1)} %maximum_bitcast_fusion), kind=kLoop, calls=%fused_computation | loop fusion | flops 25165824 | bytes 67108864 | tf_op jit(solution)/shard_map/stack | solution.py:204
  957.5 46.1 %copy.321 = f32[32,16,4,2,4,2,256]{6,5,4,3,2,1,0:T(2,128)} copy(f32[32,16,4,2,4,2,256]{6,3,0,5,1,4,2:T(2,128)} %pad_maximum_fusion) | data formatting | bytes 67108864 | tf_op jit(solution)/shard_map/stack | solution.py:204
  1003.6 39.9 %reshape.1944 = f32[32,16,64,256]{3,2,1,0:T(8,128)} reshape(f32[32,16,4,2,4,2,256]{6,5,4,3,2,1,0:T(2,128)} %copy.321) | data formatting | bytes 67108864 | tf_op jit(solution)/shard_map/reshape | solution.py:204
  1043.6 42.5 %fusion.12 = f32[32,16,64,8]{2,3,1,0:T(8,128)} fusion(f32[32,16,64,8]{2,3,1,0:T(8,128)S(1)} %bitcast.442, f32[32,16,64,256]{3,2,1,0:T(8,128)} %reshape.1944, f32[32,16,64,256]{3,2,1,0:T(8,128)} %fusion.294), kind=kOutput, calls=%fused_computation.21 | convolution fusion | flops 6446383104 | bytes 69206016 | tf_op jit(solution)/shard_map/abfz,absz->abfs/dot_general | solution.py:240
  1086.1 41.7 %fusion.13 = (f32[32,16,64,8]{2,3,1,0:T(8,128)}, f32[32,16,64,8]{2,3,1,0:T(8,128)}) fusion(f32[32,16,64,8]{2,3,1,0:T(8,128)} %get-tuple-element.128, f32[32,16,64,8]{2,3,1,0:T(8,128)S(1)} %bitcast.443, f32[32,16,64,256]{3,2,1,0:T(8,128)} %reshape.1944, f32[32,16,64,256]{3,2,1,0:T(8,128)} %select_add_fusion.1.clone.4), kind=kOutput, calls=%fused_computation.24 | convolution fusion | flops 6450315264 | bytes 71303168 | tf_op jit(solution)/shard_map/abfz,absz->abfs/dot_general | solution.py:237
  1127.9 4.9 multiply_reduce_fusion.2
  (327 shorter events, 248.0 us)
Async XLA Ops:
  10.0 3.7 copy-start.20
  13.3 7.9 copy-start.32
  13.3 7.9 copy-start.34
  13.3 7.8 copy-start.36
  13.3 7.8 copy-start.38
  13.4 7.8 copy-start.40
  13.4 7.8 copy-start.42
  13.5 3.9 copy-start.44
  13.6 3.8 copy-start.90
  17.6 4.9 copy-start.54
  17.6 4.9 copy-start.56
  17.6 4.9 copy-start.58
  17.6 4.9 copy-start.60
  17.6 4.9 copy-start.62
  17.7 4.9 copy-start.64
  361.1 8.6 collective-permute-start
  371.5 9.1 collective-permute-start.1
  451.8 55.0 %all-to-all-start.1 = ((f32[64,4,2176]{2,0,1:T(8,128)}), f32[64,4,2176]{2,0,1:T(8,128)S(1)}, u32[]{:S(2)}, u32[]{:S(2)}) async-start(f32[64,4,2176]{2,0,1:T(8,128)} %copy.297), calls=%async_computation.1 | async-start | bytes 4456448 | tf_op jit(solution)/shard_map/all_to_all | solution.py:153
  695.1 4.3 copy-start.6
  699.9 57.0 %collective-permute-start.2 = (f32[5,32,256]{2,0,1:T(8,128)S(1)}, f32[5,32,256]{2,0,1:T(8,128)S(1)}, u32[]{:S(2)}, u32[]{:S(2)}) collective-permute-start(f32[5,32,256]{2,0,1:T(8,128)S(1)} %slice.369), channel_id=1, source_target_pairs={{8,0},{16,8},{24,16},{0,24},{9,1},{17,9},{25,17},{1,25},{10,2},{18... | collective-permute-start | bytes 491528 | tf_op jit(solution)/shard_map/ppermute | solution.py:18
  757.0 111.8 %collective-permute-start.3 = (f32[70,5,256]{2,0,1:T(8,128)S(1)}, f32[70,5,256]{2,0,1:T(8,128)S(1)}, u32[]{:S(2)}, u32[]{:S(2)}) collective-permute-start(f32[70,5,256]{2,0,1:T(8,128)S(1)} %pad_maximum_fusion.10), channel_id=1, source_target_pairs={{1,0},{2,1},{3,2},{4,3},{5,4},{6,5},{7,6},{0,7},{9,8},{10,9},{11,1... | collective-permute-start | bytes 1075208 | tf_op jit(solution)/shard_map/ppermute | solution.py:18
  906.4 3.8 copy-start.2
  916.0 6.8 copy-start.10
  916.0 6.8 copy-start.11
  916.1 6.8 copy-start.12
  916.1 6.8 copy-start.14
  922.9 4.5 copy-start.8
  922.9 4.5 copy-start.13
  922.9 4.5 copy-start.15
  922.9 4.5 copy-start.17
  927.4 5.3 copy-start.7
  927.4 5.3 copy-start.16
  927.5 5.6 copy-start.18
  927.5 6.4 copy-start.19
  1003.6 39.9 %copy-start.1 = (f32[32,16,8,64]{3,2,1,0:T(8,128)S(1)}, f32[32,16,8,64]{3,2,1,0:T(8,128)}, u32[]{:S(2)}) copy-start(f32[32,16,8,64]{3,2,1,0:T(8,128)} %copy-done) | copy-start | bytes 3145732
  1086.1 41.7 %copy-start.21 = (s32[32,16,64]{2,1,0:T(8,128)S(1)}, s32[32,16,64]{2,1,0:T(8,128)}, u32[]{:S(2)}) copy-start(s32[32,16,64]{2,1,0:T(8,128)} %copy-done.20) | copy-start | bytes 393220
  1086.1 41.7 %copy-start.23 = (s32[32,16,64]{2,1,0:T(8,128)S(1)}, s32[32,16,64]{2,1,0:T(8,128)}, u32[]{:S(2)}) copy-start(s32[32,16,64]{2,1,0:T(8,128)} %copy-done.22) | copy-start | bytes 393220
  1086.1 41.7 %copy-start.25 = (s32[32,16,64]{2,1,0:T(8,128)S(1)}, s32[32,16,64]{2,1,0:T(8,128)}, u32[]{:S(2)}) copy-start(s32[32,16,64]{2,1,0:T(8,128)} %copy-done.24) | copy-start | bytes 393220
  1086.1 41.7 %copy-start.27 = (s32[32,16,64]{2,1,0:T(8,128)S(1)}, s32[32,16,64]{2,1,0:T(8,128)}, u32[]{:S(2)}) copy-start(s32[32,16,64]{2,1,0:T(8,128)} %copy-done.26) | copy-start | bytes 393220
  1086.1 41.7 %copy-start.29 = (s32[32,16,64]{2,1,0:T(8,128)S(1)}, s32[32,16,64]{2,1,0:T(8,128)}, u32[]{:S(2)}) copy-start(s32[32,16,64]{2,1,0:T(8,128)} %copy-done.28) | copy-start | bytes 393220
  1127.8 4.9 copy-start.4
  1127.8 4.9 copy-start.31
  1127.8 4.9 copy-start.83
  1127.8 4.9 copy-start.84
  1127.9 4.9 copy-start.85
  1127.9 4.9 copy-start.86
  1127.9 4.9 copy-start.87
  1127.9 4.9 copy-start.88
  (52 other events, 144.5 us)
where the time goes:
time: 1150 us; the launch traced here: 1140 us
  local copies, waits for them, and re-layouts  445 us (39%)
  matrix products  265 us (23%)
  other arithmetic  200 us (17%)
  blocking collectives  155 us (13%)
  waiting for transfers between devices  60.1 us (5%)
    dot_general x1, matrix products, local(): spread = jnp.einsum('abfs,absz->abfz', pair, weight_z, precision=highest)  141 us
    transpose x17, local copies, waits for them, and re-layouts, place_tiles(): jnp.transpose(shaped[:, :, i, :, j], (0, 2, 1, 3, 4))  86.3 us
    dot_general x2, other arithmetic, local(): jnp.einsum('abxs,abys,abxys->abs', grade_x, weight_y, main, precision=hig...  60.3 us
    reshape x16, local copies, waits for them, and re-layouts, place_tiles(): jnp.transpose(shaped[:, :, i, :, j], (0, 2, 1, 3, 4))  59.5 us
    dot_general x1, other arithmetic, local(): jnp.einsum('abfz,absz->abfs', footing, grade_z, precision=highest)  55.3 us
    all_to_all x1, blocking collectives, spectrum_pen_first(): lax.all_to_all(returning, 'grp', split_axis=0, concat_axis=1, tiled=True)  54 us
    all_to_all x1, waiting for transfers between devices, spectrum_pen_first(): lax.all_to_all(sectioned, 'grp', split_axis=1, concat_axis=0, tiled=True)  50.4 us
    reshape x16, local copies, waits for them, and re-layouts, gather_tiles(): part = part.reshape(tiles_x, 2, tiles_y, 2, KZ)  50 us
  transfers between devices with their start and end apart: 5, of which 3 were waited for; matrix products, arithmetic and copies ran while one was open for 12% of the time, Pallas kernels for 0%

commit v1 on v0

--- a/solution.py
+++ b/solution.py
@@ -10,6 +10,18 @@
 ATOMS = 1048576
 ewald_split = 0.6
 highest = lax.Precision.HIGHEST
+
+
+def split_up(value, dim, size):
+    shape = value.shape
+    pieces = value.reshape(*shape[:dim], size, shape[dim] // size, *shape[dim + 1 :])
+    return jnp.moveaxis(pieces, dim, 0)
+
+
+def in_order(pieces, dim):
+    pieces = jnp.moveaxis(pieces, 0, dim)
+    lengths = pieces.shape
+    return pieces.reshape(*lengths[:dim], lengths[dim] * lengths[dim + 1], *lengths[dim + 2 :])
 
 
 def shifted(block, axis, distance):
@@ -162,7 +174,15 @@
     scaled = jnp.stack([kernel * real_x, kernel * imag_x], axis=-1).reshape(KX, lines * planes * 2)
     real_b, imag_b = inverse_complex(scaled, cos_x, sin_x, (KX, lines, planes, 2), 3)
     returning = jnp.stack([real_b, imag_b], axis=-1).reshape(KX, lines * planes * 2)
-    rows_home = lax.all_to_all(returning, "grp", split_axis=0, concat_axis=1, tiled=True)
+    size, mine = (lax.axis_size("grp"), lax.axis_index("grp"))
+    pieces = split_up(returning, 0, size)
+    out = pieces
+    for step in range(1, size):
+        target, source = ((mine + step) % size, (mine - step) % size)
+        sent = lax.dynamic_index_in_dim(pieces, target, 0)
+        received = lax.ppermute(sent, "grp", [(i_2, (i_2 + step) % size) for i_2 in range(size)])
+        out = lax.dynamic_update_slice_in_dim(out, received, source, axis=0)
+    rows_home = in_order(out, 1)
     rows_home = jnp.transpose(rows_home.reshape(block_x, KY, planes, 2), (1, 2, 3, 0)).reshape(
         KY, planes * 2 * block_x
     )

time: 1150 us -> 1240 us (1.078)
  local copies, waits for them, and re-layouts: 445 us -> 550 us
  blocking collectives: 155 us -> 121 us
    dynamic_update_slice x0 -> x3, local copies, waits for them, and re-layouts: none -> 89.5 us  [spectrum_pen_first(): out = lax.dynamic_update_slice_in_dim(out, received, source, axis=0)]
    all_to_all x1 -> x0, blocking collectives: 54 us -> none  [spectrum_pen_first(): lax.all_to_all(returning, 'grp', split_axis=0, concat_axis=1, tiled=True)]
    psum x1, blocking collectives: 38.4 us -> 58.6 us  [local(): total = lax.psum(spectral, ('grp', 'pen'))]
    all_to_all x3 -> x0, local copies, waits for them, and re-layouts: 14.1 us -> none  [spectrum_pen_first(): lax.all_to_all(returning, 'grp', split_axis=0, concat_axis=1, tiled=True)]
    dynamic_slice x0 -> x4, local copies, waits for them, and re-layouts: none -> 13 us  [spectrum_pen_first(): sent = lax.dynamic_index_in_dim(pieces, target, 0)]
  transfers between devices with their start and end apart: 5 -> 8, of which waited for: 3 -> 4; matrix products, arithmetic and copies ran while one was open for 12% -> 16% of each run, Pallas kernels for 0% -> 0%
where the time goes in v1:
time: 1240 us; the launch traced here: 1220 us
  local copies, waits for them, and re-layouts  550 us (44%)
  matrix products  265 us (21%)
  other arithmetic  201 us (16%)
  blocking collectives  121 us (10%)
  waiting for transfers between devices  71.1 us (6%)
    dot_general x1, matrix products, local(): spread = jnp.einsum('abfs,absz->abfz', pair, weight_z, precision=highest)  141 us
    dynamic_update_slice x3, local copies, waits for them, and re-layouts, spectrum_pen_first(): out = lax.dynamic_update_slice_in_dim(out, received, source, axis=0)  89.5 us
    transpose x17, local copies, waits for them, and re-layouts, place_tiles(): jnp.transpose(shaped[:, :, i, :, j], (0, 2, 1, 3, 4))  86.4 us
    dot_general x2, other arithmetic, local(): jnp.einsum('abxs,abys,abxys->abs', grade_x, weight_y, main, precision=hig...  60.1 us
    reshape x16, local copies, waits for them, and re-layouts, place_tiles(): jnp.transpose(shaped[:, :, i, :, j], (0, 2, 1, 3, 4))  59.6 us
    psum x1, blocking collectives, local(): total = lax.psum(spectral, ('grp', 'pen'))  58.6 us
    dot_general x1, other arithmetic, local(): jnp.einsum('abfz,absz->abfs', footing, grade_z, precision=highest)  55.3 us
    all_to_all x1, waiting for transfers between devices, spectrum_pen_first(): lax.all_to_all(sectioned, 'grp', split_axis=1, concat_axis=0, tiled=True)  50.4 us
  transfers between devices with their start and end apart: 8, of which 4 were waited for; matrix products, arithmetic and copies ran while one was open for 16% of the time, Pallas kernels for 0%

profile of v1, /device:TPU:0, one launch (start us, length us, event | category | flops | bytes accessed | tf_op | source)
XLA Modules:
  0.0 1223.8 jit_solution(4078929496152658713)
XLA Ops:
  23.0 140.7 %fusion.15 = f32[32,16,64,256]{3,2,1,0:T(8,128)} fusion(f32[32,16,64]{2,1,0:T(8,128)S(1)} %copy-done.60, s32[32,16,64]{2,1,0:T(8,128)S(1)} %get-tuple-element.187, f32[32,16,64]{2,1,0:T(8,128)S(1)} %copy-done.58, s32[32,16,64]{2,1,0:T(8,128)S(1)} %get-tuple-element.186, f32[32,16,64]{2,1,0:T(8,128)S(1)} %copy-done.54, ...), kind=kOutput, calls=%fused_computation.27 | convolution fusion | flops 6589251584 | bytes 37355520 | tf_op jit(solution)/shard_map/abfs,absz->abfz/dot_general | solution.py:243
  163.7 39.0 %reshape.1898 = f32[32,16,4,2,4,2,256]{6,5,4,3,2,1,0:T(2,128)} reshape(f32[32,16,64,256]{3,2,1,0:T(8,128)} %fusion.15) | data formatting | bytes 67108864 | tf_op jit(solution)/shard_map/reshape | solution.py:204
  202.7 25.2 %slice_bitcast_fusion.15 = (f32[32,2,16,2,256]{4,3,1,2,0:T(2,128)S(1)}, f32[32,2,16,2,256]{4,3,1,2,0:T(2,128)S(1)}, f32[32,2,16,2,256]{4,3,1,2,0:T(2,128)}, f32[...) fusion(f32[32,16,4,2,4,2,256]{6,5,4,3,2,1,0:T(2,128)} %reshape.1898), kind=kLoop, calls=%fused_computation.93 | loop fusion | bytes 67108864 | tf_op jit(solution)/shard_map/transpose | solution.py:208
  241.7 4.1 copy.291
  257.3 4.1 copy.293
  319.2 4.1 copy.301
  348.8 12.9 %pad_add_fusion = f32[70,38,256]{2,0,1:T(8,128)S(1)} fusion(f32[64,32,256]{2,0,1:T(8,128)} %reshape.1914, f32[64,32,256]{2,0,1:T(8,128)} %reshape.1913, f32[64,32,256]{2,0,1:T(8,128)} %reshape.1912, f32[64,32,256]{2,0,1:T(8,128)} %reshape.1911, f32[64,32,256]{2,0,1:T(8,128)} %reshape.1910, f32[64,32,256]{2,0,1:T(8,128)} %reshape.1909, ...), kind=kLoop, calls=%fused_computation.52 | loop fusion | flops 10214400 | bytes 36278272 | tf_op jit(solution)/shard_map/add | solution.py:211
  365.7 4.7 collective-permute-done
  376.4 5.0 collective-permute-done.1
  389.7 7.5 copy.305
  397.3 4.6 all_to_all.40
  402.3 31.3 %all_to_all.54 = f32[32,8,2176]{2,0,1:T(8,128)} all-to-all(f32[32,8,2176]{2,0,1:T(8,128)S(1)} %copy.306), channel_id=1, replica_groups=mesh['grp'=4,'pen'=8] {'pen'}, dimensions={1} | all-to-all | bytes 4456448 | tf_op jit(solution)/shard_map/all_to_all | solution.py:160
  442.3 5.0 copy.311
  447.3 5.1 copy.312
  456.9 50.4 %all-to-all-done.1 = f32[64,4,2176]{2,0,1:T(8,128)S(1)} async-done(((f32[64,4,2176]{2,0,1:T(8,128)}), f32[64,4,2176]{2,0,1:T(8,128)S(1)}, u32[]{:S(2)}, u32[]{:S(2)}) %all-to-all-start.1) | async-done | bytes 2228256 | tf_op jit(solution)/shard_map/all_to_all | solution.py:165
  536.0 4.8 reshape_reshape.6
  540.8 8.2 constant_dynamic-slice_fusion.2
  557.8 11.1 collective-permute-done.2
  571.9 29.8 %dynamic_update_slice.9 = f32[4,64,2176]{1,0,2:T(4,128)} dynamic-update-slice(f32[4,64,2176]{1,0,2:T(4,128)} %reshape_reshape.6, f32[1,64,2176]{1,0,2:T(1,128)S(1)} %copy.327, s32[]{:T(128)S(6)} %select_n.427, s32[]{:T(128)} %constant.649.clone.1, s32[]{:T(128)} %constant.649.clone.1) | dynamic-update-slice | bytes 1114116 | tf_op jit(solution)/shard_map/dynamic_update_slice | solution.py:184
  603.1 29.8 %dynamic_update_slice.10 = f32[4,64,2176]{1,0,2:T(4,128)} dynamic-update-slice(f32[4,64,2176]{1,0,2:T(4,128)} %dynamic_update_slice.9, f32[1,64,2176]{1,0,2:T(1,128)S(1)} %copy.329, s32[]{:T(128)S(6)} %select_n.431, s32[]{:T(128)} %constant.649.clone.1, s32[]{:T(128)} %constant.649.clone.1) | dynamic-update-slice | bytes 1114116 | tf_op jit(solution)/shard_map/dynamic_update_slice | solution.py:184
  634.4 29.8 %dynamic_update_slice.11 = f32[4,64,2176]{1,0,2:T(4,128)} dynamic-update-slice(f32[4,64,2176]{1,0,2:T(4,128)} %dynamic_update_slice.10, f32[1,64,2176]{1,0,2:T(1,128)S(1)} %copy.331, s32[]{:T(128)S(6)} %select_n.435, s32[]{:T(128)} %constant.649.clone.1, s32[]{:T(128)} %constant.649.clone.1) | dynamic-update-slice | bytes 1114116 | tf_op jit(solution)/shard_map/dynamic_update_slice | solution.py:184
  664.2 4.6 copy.332
  668.9 7.1 copy.392
  675.9 6.1 copy.333
  682.1 4.6 fusion.36
  690.3 5.0 copy.337
  695.3 4.6 all_to_all.48
  700.0 30.8 %all_to_all.55 = f32[8,32,2176]{2,1,0:T(8,128)S(1)} all-to-all(f32[8,32,2176]{2,1,0:T(8,128)S(1)} %all_to_all.48), channel_id=1, replica_groups=mesh['grp'=4,'pen'=8] {'pen'}, dimensions={0} | all-to-all | bytes 4456448 | tf_op jit(solution)/shard_map/all_to_all | solution.py:191
  732.1 4.1 reshape.1917
  736.2 8.8 fusion.280
  745.0 5.8 copy.398
  750.8 5.3 fusion.141
  756.1 4.3 copy.397
  760.4 4.2 fusion.143
  766.5 55.3 %select_add_fusion.1.clone.4 = f32[32,16,64,256]{3,2,1,0:T(8,128)} fusion(f32[32,16,64]{2,1,0:T(8,128)S(1)} %copy-done.61, s32[32,16,64]{2,1,0:T(8,128)S(1)} %copy-done.43, f32[32,16,64]{2,1,0:T(8,128)S(1)} %copy-done.59, s32[32,16,64]{2,1,0:T(8,128)S(1)} %copy-done.41, f32[32,16,64]{2,1,0:T(8,128)S(1)} %copy-done.55, ...), kind=kLoop, calls=%fused_computation.13.clone.clone.clone.clone.1 | loop fusion | flops 142606336 | bytes 35127296 | tf_op jit(solution)/shard_map/abxs,abys,abxys->abs/dot_general | solution.py:263
  823.1 55.3 %fusion.294 = f32[32,16,64,256]{3,2,1,0:T(8,128)} fusion(f32[32,16,64]{2,1,0:T(8,128)S(1)} %copy-done.53, f32[32,16,64]{2,1,0:T(8,128)S(1)} %copy-done.51, f32[32,16,64]{2,1,0:T(8,128)S(1)} %copy-done.50, f32[32,16,64]{2,1,0:T(8,128)S(1)} %copy-done.52, f32[32,16,64]{2,1,0:T(8,128)S(1)} %copy-done.49, f32[32,16,64]{2,1,0:T(8,128)S(1)} %copy-done.48, ...), kind=kLoop, calls=%fused_computation.2.clone.clone.clone.1 | loop fusion | flops 142606336 | bytes 35127296 | tf_op jit(solution)/shard_map/abfz,absz->abfs/dot_general | solution.py:260
  879.2 58.6 %psum.7 = f32[]{:T(128)} all-reduce(f32[]{:T(128)S(6)} %mul_shard_map.3), channel_id=1, replica_groups=mesh['grp'=4,'pen'=8] {'grp','pen'}, use_global_device_ids=true, to_apply=%region_1.6 | all-reduce | flops 1 | bytes 8 | tf_op jit(solution)/shard_map/psum | solution.py:272
  954.2 6.2 fusion.282
  1001.1 6.8 maximum_bitcast_fusion
  1008.0 4.5 maximum_bitcast_fusion.1
  1012.5 5.3 maximum_bitcast_fusion.2
  1018.9 5.2 maximum_bitcast_fusion.3
  1024.1 18.5 %pad_maximum_fusion = f32[32,16,4,2,4,2,256]{6,3,0,5,1,4,2:T(2,128)} fusion(f32[32,16,1,2,4,2,256]{6,3,0,5,1,4,2:T(2,128)} %maximum_bitcast_fusion.3, f32[32,16,1,2,4,2,256]{6,3,0,5,1,4,2:T(2,128)} %maximum_bitcast_fusion.2, f32[32,16,1,2,4,2,256]{6,3,0,5,1,4,2:T(2,128)S(1)} %maximum_bitcast_fusion.1, f32[32,16,1,2,4,2,256]{6,3,0,5,1,4,2:T(2,128)S(1)} %maximum_bitcast_fusion), kind=kLoop, calls=%fused_computation | loop fusion | flops 25165824 | bytes 67108864 | tf_op jit(solution)/shard_map/stack | solution.py:224
  1042.6 46.1 %copy.341 = f32[32,16,4,2,4,2,256]{6,5,4,3,2,1,0:T(2,128)} copy(f32[32,16,4,2,4,2,256]{6,3,0,5,1,4,2:T(2,128)} %pad_maximum_fusion) | data formatting | bytes 67108864 | tf_op jit(solution)/shard_map/stack | solution.py:224
  1088.7 39.9 %reshape.1934 = f32[32,16,64,256]{3,2,1,0:T(8,128)} reshape(f32[32,16,4,2,4,2,256]{6,5,4,3,2,1,0:T(2,128)} %copy.341) | data formatting | bytes 67108864 | tf_op jit(solution)/shard_map/reshape | solution.py:224
  1128.7 42.5 %fusion.12 = f32[32,16,64,8]{2,3,1,0:T(8,128)} fusion(f32[32,16,64,8]{2,3,1,0:T(8,128)S(1)} %bitcast.443, f32[32,16,64,256]{3,2,1,0:T(8,128)} %reshape.1934, f32[32,16,64,256]{3,2,1,0:T(8,128)} %fusion.294), kind=kOutput, calls=%fused_computation.21 | convolution fusion | flops 6446383104 | bytes 69206016 | tf_op jit(solution)/shard_map/abfz,absz->abfs/dot_general | solution.py:260
  1171.1 41.7 %fusion.13 = (f32[32,16,64,8]{2,3,1,0:T(8,128)}, f32[32,16,64,8]{2,3,1,0:T(8,128)}) fusion(f32[32,16,64,8]{2,3,1,0:T(8,128)} %get-tuple-element.131, f32[32,16,64,8]{2,3,1,0:T(8,128)S(1)} %bitcast.444, f32[32,16,64,256]{3,2,1,0:T(8,128)} %reshape.1934, f32[32,16,64,256]{3,2,1,0:T(8,128)} %select_add_fusion.1.clone.4), kind=kOutput, calls=%fused_computation.24 | convolution fusion | flops 6450315264 | bytes 71303168 | tf_op jit(solution)/shard_map/abfz,absz->abfs/dot_general | solution.py:257
  1212.9 4.9 multiply_reduce_fusion.2
  (341 shorter events, 275.4 us)
Async XLA Ops:
  13.4 8.2 copy-start.32
  13.4 8.2 copy-start.34
  13.4 8.2 copy-start.36
  13.4 8.2 copy-start.38
  13.4 8.2 copy-start.40
  13.4 8.2 copy-start.42
  13.5 4.3 copy-start.44
  13.6 4.3 copy-start.90
  18.1 4.9 copy-start.54
  18.1 4.9 copy-start.56
  18.1 4.9 copy-start.58
  18.1 4.9 copy-start.60
  18.1 4.9 copy-start.62
  18.1 4.9 copy-start.64
  361.7 8.6 collective-permute-start
  372.1 9.2 collective-permute-start.1
  452.5 54.8 %all-to-all-start.1 = ((f32[64,4,2176]{2,0,1:T(8,128)}), f32[64,4,2176]{2,0,1:T(8,128)S(1)}, u32[]{:S(2)}, u32[]{:S(2)}) async-start(f32[64,4,2176]{2,0,1:T(8,128)} %copy.312), calls=%async_computation.1 | async-start | bytes 4456448 | tf_op jit(solution)/shard_map/all_to_all | solution.py:165
  551.2 17.7 %collective-permute-start.2 = (f32[1,64,2176]{2,1,0:T(8,128)}, f32[1,64,2176]{2,1,0:T(8,128)}, u32[]{:S(2)}, u32[]{:S(2)}) collective-permute-start(f32[1,64,2176]{2,1,0:T(8,128)} %copy.326), channel_id=1, source_target_pairs={{0,8},{8,16},{16,24},{24,0},{1,9},{9,17},{17,25},{25,1},{2,10},{10... | collective-permute-start | bytes 1671176 | tf_op jit(solution)/shard_map/ppermute | solution.py:183
  552.5 49.2 %collective-permute-start.3 = (f32[1,64,2176]{2,1,0:T(8,128)S(1)}, f32[1,64,2176]{2,1,0:T(8,128)S(1)}, u32[]{:S(2)}, u32[]{:S(2)}) collective-permute-start(f32[1,64,2176]{2,1,0:T(8,128)S(1)} %copy.328), channel_id=1, source_target_pairs={{0,16},{8,24},{16,0},{24,8},{1,17},{9,25},{17,1},{25,9},{2,18},{10... | collective-permute-start | bytes 1671176 | tf_op jit(solution)/shard_map/ppermute | solution.py:183
  555.9 77.1 %collective-permute-start.4 = (f32[1,64,2176]{2,1,0:T(8,128)S(1)}, f32[1,64,2176]{2,1,0:T(8,128)S(1)}, u32[]{:S(2)}, u32[]{:S(2)}) collective-permute-start(f32[1,64,2176]{2,1,0:T(8,128)S(1)} %copy.330), channel_id=1, source_target_pairs={{0,24},{8,0},{16,8},{24,16},{1,25},{9,1},{17,9},{25,17},{2,26},{10... | collective-permute-start | bytes 1671176 | tf_op jit(solution)/shard_map/ppermute | solution.py:183
  765.2 56.6 %collective-permute-start.5 = (f32[5,32,256]{2,0,1:T(8,128)S(1)}, f32[5,32,256]{2,0,1:T(8,128)S(1)}, u32[]{:S(2)}, u32[]{:S(2)}) collective-permute-start(f32[5,32,256]{2,0,1:T(8,128)S(1)} %slice.369), channel_id=1, source_target_pairs={{8,0},{16,8},{24,16},{0,24},{9,1},{17,9},{25,17},{1,25},{10,2},{18... | collective-permute-start | bytes 491528 | tf_op jit(solution)/shard_map/ppermute | solution.py:30
  821.9 132.0 %collective-permute-start.6 = (f32[70,5,256]{2,0,1:T(8,128)S(1)}, f32[70,5,256]{2,0,1:T(8,128)S(1)}, u32[]{:S(2)}, u32[]{:S(2)}) collective-permute-start(f32[70,5,256]{2,0,1:T(8,128)S(1)} %pad_maximum_fusion.10), channel_id=1, source_target_pairs={{1,0},{2,1},{3,2},{4,3},{5,4},{6,5},{7,6},{0,7},{9,8},{10,9},{11,1... | collective-permute-start | bytes 1075208 | tf_op jit(solution)/shard_map/ppermute | solution.py:30
  1001.1 6.8 copy-start.10
  1001.1 6.8 copy-start.11
  1001.1 6.8 copy-start.12
  1001.1 6.8 copy-start.14
  1007.9 4.5 copy-start.8
  1007.9 4.5 copy-start.13
  1008.0 4.5 copy-start.15
  1008.0 4.5 copy-start.17
  1012.5 5.3 copy-start.7
  1012.5 5.3 copy-start.16
  1012.5 5.6 copy-start.18
  1012.5 6.4 copy-start.19
  1088.7 39.9 %copy-start.1 = (f32[32,16,8,64]{3,2,1,0:T(8,128)S(1)}, f32[32,16,8,64]{3,2,1,0:T(8,128)}, u32[]{:S(2)}) copy-start(f32[32,16,8,64]{3,2,1,0:T(8,128)} %copy-done) | copy-start | bytes 3145732
  1171.1 41.7 %copy-start.21 = (s32[32,16,64]{2,1,0:T(8,128)S(1)}, s32[32,16,64]{2,1,0:T(8,128)}, u32[]{:S(2)}) copy-start(s32[32,16,64]{2,1,0:T(8,128)} %copy-done.20) | copy-start | bytes 393220
  1171.1 41.7 %copy-start.23 = (s32[32,16,64]{2,1,0:T(8,128)S(1)}, s32[32,16,64]{2,1,0:T(8,128)}, u32[]{:S(2)}) copy-start(s32[32,16,64]{2,1,0:T(8,128)} %copy-done.22) | copy-start | bytes 393220
  1171.1 41.7 %copy-start.25 = (s32[32,16,64]{2,1,0:T(8,128)S(1)}, s32[32,16,64]{2,1,0:T(8,128)}, u32[]{:S(2)}) copy-start(s32[32,16,64]{2,1,0:T(8,128)} %copy-done.24) | copy-start | bytes 393220
  1171.1 41.7 %copy-start.27 = (s32[32,16,64]{2,1,0:T(8,128)S(1)}, s32[32,16,64]{2,1,0:T(8,128)}, u32[]{:S(2)}) copy-start(s32[32,16,64]{2,1,0:T(8,128)} %copy-done.26) | copy-start | bytes 393220
  1171.1 41.7 %copy-start.29 = (s32[32,16,64]{2,1,0:T(8,128)S(1)}, s32[32,16,64]{2,1,0:T(8,128)}, u32[]{:S(2)}) copy-start(s32[32,16,64]{2,1,0:T(8,128)} %copy-done.28) | copy-start | bytes 393220
  1212.8 4.9 copy-start.4
  1212.9 4.9 copy-start.31
  1212.9 4.9 copy-start.83
  1212.9 4.9 copy-start.84
  1212.9 4.9 copy-start.85
  1212.9 4.9 copy-start.86
  1212.9 4.9 copy-start.87
  1212.9 4.9 copy-start.88
  (55 other events, 155.7 us)
